TPU v7x, 32 devices: a whole 2x2x4 slice. The times are simulated.
32 devices in a mesh: sub: 8 (over z, x), blk: 4 (over y, core).
Axes of the slice: x: 2, y: 2, z: 4, core: 2. Of those that a mesh axis runs over, the one named last changes fastest.
Arguments:
- coefficients: float32 [512, 4, 2, 64, 128], P('sub', None, None, 'blk'), may hold values from -0.2 to 0.2
- owner_slot: int32 [512], P('sub'), may hold values from 0 to 511, as said below
- child_list: int32 [512, 8], P('sub'), may hold values from 0 to 7, each once within a row
Outputs:
- children: float32 [512, 4, 8, 64, 2, 128], P('sub', None, None, 'blk')
Inputs may be any that keep to these rules, and one draw needn't show every extreme that they name: owner_slot is a permutation of the 512 positions; position s belongs to subtree index s // 64; of the 64 boxes held by one subtree index exactly 8 belong to each subtree index. `child_list`: each row lists the 8 octant codes once each.
All inputs are finite; a program needn't handle non-finite values.
Results may differ from a plain program's by a relative error of at most 0.0003.
Values sent between devices are 32-bit elements; how exact they have to be, the bound alone decides.
A program may use at most 128 MiB of HBM per device.

v0:
```python
import jax
import jax.numpy as jnp
from jax import lax
from jax.sharding import PartitionSpec as P

L = 64
M = 128
J = 64
K = 128


def legendre_table(orders_abs, polar, degrees):
    cosines = jnp.cos(polar)[None, :]
    sines = jnp.sin(polar)[None, :]
    order_col = orders_abs[:, None]
    log_start = 0.5 * (
        jnp.log((2.0 * order_col + 1.0) / (4.0 * jnp.pi))
        + lax.lgamma(2.0 * order_col + 1.0)
        - order_col * jnp.log(4.0)
        - 2.0 * lax.lgamma(order_col + 1.0)
    ) + order_col * jnp.log(sines)
    diag_value = jnp.exp(log_start)
    next_value = jnp.sqrt(2.0 * order_col + 3.0) * cosines * diag_value

    def advance(state, degree):
        previous, before, factor_prev = state
        numer = jnp.maximum(4.0 * degree * degree - 1.0, 1.0)
        denom = jnp.maximum(degree * degree - order_col * order_col, 1.0)
        factor = jnp.sqrt(numer / denom)
        recur = factor * (cosines * previous - before / factor_prev)
        value = jnp.where(
            degree < order_col,
            0.0,
            jnp.where(
                degree == order_col,
                diag_value,
                jnp.where(degree == order_col + 1.0, next_value, recur),
            ),
        )
        return ((value, previous, factor), value)

    zeros = jnp.zeros_like(diag_value)
    start_state = (zeros, zeros, jnp.ones_like(order_col))
    _, values = lax.scan(advance, start_state, jnp.arange(degrees).astype(jnp.float32))
    return values


def dft_table(degrees, columns, azimuths):
    column_ids = jnp.arange(columns, dtype=jnp.int32)
    azimuth_ids = jnp.arange(azimuths, dtype=jnp.int32)
    turns = jnp.mod((column_ids[:, None] - degrees) * azimuth_ids[None, :], azimuths)
    angle = 2.0 * jnp.pi * turns.astype(jnp.float32) / azimuths
    cosine = jnp.cos(angle)
    sine = jnp.sin(angle)
    upper = jnp.concatenate([cosine, sine], axis=1)
    lower = jnp.concatenate([-sine, cosine], axis=1)
    return jnp.concatenate([upper, lower], axis=0)


def shift_children(waves, octants, polar, azimuths):
    azimuth = 2.0 * jnp.pi * jnp.arange(azimuths).astype(jnp.float32) / azimuths
    dir_x = jnp.sin(polar)[:, None] * jnp.cos(azimuth)[None, :]
    dir_y = jnp.sin(polar)[:, None] * jnp.sin(azimuth)[None, :]
    dir_z = jnp.cos(polar)[:, None] * jnp.ones_like(azimuth)[None, :]
    sign_x = (2 * (octants & 1) - 1).astype(jnp.float32)[:, None, None]
    sign_y = (2 * (octants >> 1 & 1) - 1).astype(jnp.float32)[:, None, None]
    sign_z = (2 * (octants >> 2 & 1) - 1).astype(jnp.float32)[:, None, None]
    phase = 5.5 * (sign_x * dir_x[None] + sign_y * dir_y[None] + sign_z * dir_z[None])
    phase_cos = jnp.cos(phase)[None]
    phase_sin = jnp.sin(phase)[None]
    wave_re = waves[:, :, 0, :][:, None]
    wave_im = waves[:, :, 1, :][:, None]
    real_part = wave_re * phase_cos - wave_im * phase_sin
    imag_part = wave_re * phase_sin + wave_im * phase_cos
    return jnp.stack([real_part, imag_part], axis=-2)


def body(coefficients, owner_slot, child_list):
    box_count = coefficients.shape[0]
    cases = coefficients.shape[1]
    sub_count = lax.axis_size("sub")
    per_peer = box_count // sub_count
    targets = owner_slot // box_count
    positions = owner_slot % box_count
    send_order = jnp.argsort(targets, stable=True)
    outgoing = coefficients[send_order].reshape((sub_count, per_peer) + coefficients.shape[1:])
    placed = positions[send_order].reshape(sub_count, per_peer)
    arrived, arrived_slots = (
        lax.all_to_all(outgoing, "sub", split_axis=0, concat_axis=0, tiled=True),
        lax.all_to_all(placed, "sub", split_axis=0, concat_axis=0, tiled=True),
    )
    restore = jnp.argsort(arrived_slots.reshape(-1))
    owned = arrived.reshape(coefficients.shape)[restore]
    blk_count = lax.axis_size("blk")
    blk_index = lax.axis_index("blk")
    cycle_width = J // blk_count
    polar_all = jnp.pi * (jnp.arange(J).astype(jnp.float32) + 0.5) / J
    polar_mine = lax.dynamic_slice_in_dim(polar_all, blk_index * cycle_width, cycle_width, 0)
    spectral = dft_table(L, M, K)
    orders_abs = jnp.abs(jnp.arange(M, dtype=jnp.int32) - L).astype(jnp.float32)
    table = legendre_table(orders_abs, polar_all, L)
    my_boxes = lax.all_to_all(owned, "blk", split_axis=0, concat_axis=3, tiled=True)
    box_share = my_boxes.shape[0]
    cycles = jnp.einsum("brxlc,lcj->brjxc", my_boxes, table, precision=lax.Precision.HIGHEST)
    spectra = jnp.dot(
        cycles.reshape(box_share * cases * J, 2 * M), spectral, precision=lax.Precision.HIGHEST
    )
    spectra = spectra.reshape(box_share, cases, J, 2, K)
    waves = lax.all_to_all(spectra, "blk", split_axis=2, concat_axis=0, tiled=True)
    return jax.vmap(shift_children, in_axes=(0, 0, None, None))(waves, child_list, polar_mine, K)


def solution(mesh):
    placed = (P("sub", None, None, "blk", None), P("sub"), P("sub", None))
    return jax.shard_map(
        body,
        mesh=mesh,
        in_specs=placed,
        out_specs=P("sub", None, None, "blk", None, None),
        check_vma=False,
    )
```

profile of v0, /device:TPU:11, one launch (start us, length us, event | category | flops | bytes accessed | tf_op | source)
XLA Modules:
  0.0 644.0 jit_solution(16657285089696735481)
XLA Ops:
  0.7 2.0 sort.34
  4.2 5.7 all-to-all-start.1
  9.8 5.0 gather_fusion
  14.9 5.4 all-to-all-start
  21.7 2.1 sort.35
  23.8 87.2 %all-to-all-done = f32[8,8,4,2,16,128]{5,4,3,2,1,0:T(8,128)} async-done(((f32[8,8,4,2,16,128]{5,4,3,2,1,0:T(8,128)}), f32[8,8,4,2,16,128]{5,4,3,2,1,0:T(8,128)}, u32[]{:S(2)}, u32[]{:S(2)}) %all-to-all-start) | async-done | bytes 4194336 | tf_op jit(solution)/shard_map/all_to_all | solution.py:89
  110.9 5.0 gather_fusion.2
  116.0 5.3 all-to-all-start.2
  121.3 335.6 %while.22 = (s32[]{:T(128)}, f32[128,64]{1,0:T(8,128)S(1)}, f32[128,64]{1,0:T(8,128)S(1)}, f32[128,1]{0,1:T(1,128)S(1)}, f32[64,128,64]{2,1,0:T(8,128)}, /*index...) while((s32[]{:T(128)}, f32[128,64]{1,0:T(8,128)S(1)}, ...), condition=%wide.region_1.2_spmd.clone.clone.clone.clone, body=%wide.region_0.1_spmd.clone.clone.clone.clone.sunk | while | flops 101704 | bytes 203276 | solution.py:44
  125.7 0.8 bitcast_dynamic-update-slice_fusion.2
  146.6 0.8 bitcast_dynamic-update-slice_fusion.2
  157.1 0.8 bitcast_dynamic-update-slice_fusion.2
  162.3 0.8 bitcast_dynamic-update-slice_fusion.2
  167.6 0.8 bitcast_dynamic-update-slice_fusion.2
  172.8 0.8 bitcast_dynamic-update-slice_fusion.2
  178.1 0.9 bitcast_dynamic-update-slice_fusion.2
  183.3 0.8 bitcast_dynamic-update-slice_fusion.2
  188.6 0.8 bitcast_dynamic-update-slice_fusion.2
  193.8 0.8 bitcast_dynamic-update-slice_fusion.2
  209.6 0.8 bitcast_dynamic-update-slice_fusion.2
  214.8 0.8 bitcast_dynamic-update-slice_fusion.2
  220.1 0.8 bitcast_dynamic-update-slice_fusion.2
  230.5 0.8 bitcast_dynamic-update-slice_fusion.2
  235.8 0.8 bitcast_dynamic-update-slice_fusion.2
  251.5 0.8 bitcast_dynamic-update-slice_fusion.2
  262.0 0.8 bitcast_dynamic-update-slice_fusion.2
  267.2 0.8 bitcast_dynamic-update-slice_fusion.2
  277.7 0.8 bitcast_dynamic-update-slice_fusion.2
  288.2 0.8 bitcast_dynamic-update-slice_fusion.2
  293.4 0.8 bitcast_dynamic-update-slice_fusion.2
  303.9 0.8 bitcast_dynamic-update-slice_fusion.2
  309.2 0.8 bitcast_dynamic-update-slice_fusion.2
  319.7 0.8 bitcast_dynamic-update-slice_fusion.2
  335.4 0.8 bitcast_dynamic-update-slice_fusion.2
  340.6 0.8 bitcast_dynamic-update-slice_fusion.2
  345.9 0.8 bitcast_dynamic-update-slice_fusion.2
  351.1 0.8 bitcast_dynamic-update-slice_fusion.2
  356.4 0.8 bitcast_dynamic-update-slice_fusion.2
  377.3 0.8 bitcast_dynamic-update-slice_fusion.2
  393.0 0.8 bitcast_dynamic-update-slice_fusion.2
  398.3 0.9 bitcast_dynamic-update-slice_fusion.2
  408.7 0.8 bitcast_dynamic-update-slice_fusion.2
  414.0 0.8 bitcast_dynamic-update-slice_fusion.2
  419.2 0.8 bitcast_dynamic-update-slice_fusion.2
  429.7 0.8 bitcast_dynamic-update-slice_fusion.2
  440.2 0.8 bitcast_dynamic-update-slice_fusion.2
  445.5 0.9 bitcast_dynamic-update-slice_fusion.2
  450.7 0.8 bitcast_dynamic-update-slice_fusion.2
  456.0 0.8 bitcast_dynamic-update-slice_fusion.2
  457.1 4.8 copy.26
  461.9 9.1 %copy.28 = f32[16,4,2,64,128]{3,0,2,1,4:T(8,128)} copy(f32[16,4,2,64,128]{4,3,2,1,0:T(8,128)} %bitcast.59) | data formatting | bytes 8388608 | tf_op jit(solution)/shard_map/all_to_all | solution.py:102
  471.1 15.5 %fusion.24 = f32[16,4,64,2,128]{2,0,3,1,4:T(8,128)} fusion(f32[16,4,2,64,128]{3,0,2,1,4:T(8,128)} %copy.28, f32[64,128,64,1,1]{2,1,0,4,3:T(8,128)} %bitcast.63), kind=kOutput, calls=%fused_computation.37 | convolution fusion | flops 805306368 | bytes 10485760 | tf_op jit(solution)/shard_map/brxlc,lcj->brjxc/dot_general | solution.py:104
  486.5 9.0 %copy.29 = f32[16,4,64,2,128]{4,3,2,1,0:T(2,128)} copy(f32[16,4,64,2,128]{2,0,3,1,4:T(8,128)} %fusion.24) | data formatting | bytes 8388608 | tf_op jit(solution)/shard_map/brxlc,lcj->brjxc/transpose | solution.py:104
  495.5 6.4 reshape.499
  501.9 6.0 fusion.18
  508.0 5.2 copy.30
  513.2 5.0 all-to-all-start.3
  518.8 17.3 %fusion.23 = (f32[64,8,16,128]{3,2,1,0:T(8,128)}, f32[64,8,16,128]{3,2,1,0:T(8,128)}) fusion(f32[16]{0:T(128)S(1)} %get-tuple-element.345, f32[64,8]{1,0:T(8,128)S(1)} %copy.35, f32[16,128]{1,0:T(8,128)S(1)} %get-tuple-element.343, f32[64,8]{1,0:T(8,128)S(1)} %copy.34, f32[16,128]{1,0:T(8,128)S(1)} %get-tuple-element.342, f32[64,8]{1,0:T(8,128)S(1)} %copy.33), kind=kLoop, calls=%fused_computation.36 | loop fusion | flops 6291456 | bytes 8411200 | tf_op jit(solution)/shard_map/vmap()/cos | solution.py:69
  536.0 29.5 %all-to-all-done.3 = f32[16,4,64,2,128]{4,3,1,0,2:T(2,128)} async-done(((f32[16,4,64,2,128]{4,3,1,0,2:T(2,128)}), f32[16,4,64,2,128]{4,3,1,0,2:T(2,128)}, u32[]{:S(2)}, u32[]{:S(2)}) %all-to-all-start.3) | async-done | bytes 4194336 | tf_op jit(solution)/shard_map/all_to_all | solution.py:109
  565.5 4.6 copy.31
  571.4 1.5 copy-done
  573.0 1.3 copy-done.1
  574.2 36.9 %multiply_subtract_fusion.1 = (f32[64,4,8,16,1,128]{5,4,3,2,1,0:T(1,128)}, f32[64,4,8,16,1,128]{5,4,3,2,1,0:T(1,128)}) fusion(f32[64,8,16,128]{3,2,1,0:T(8,128)S(1)} %copy-done.1, f32[64,4,16,128]{3,2,1,0:T(8,128)S(1)} %get-tuple-element.331, f32[64,8,16,128]{3,2,1,0:T(8,128)S(1)} %copy-done, f32[64,4,16,128]{3,2,1,0:T(8,128)S(1)} %get-tuple-element.330), kind=kLoop, calls=%fused_computation.29 | loop fusion | flops 25165824 | bytes 46137344 | tf_op jit(solution)/shard_map/vmap()/sub | solution.py:73
  611.1 32.8 %pad_maximum_fusion = f32[64,4,8,16,2,128]{5,4,3,2,1,0:T(2,128)} fusion(f32[64,4,8,16,1,128]{5,4,3,2,1,0:T(1,128)} %get-tuple-element.329, f32[64,4,8,16,1,128]{5,4,3,2,1,0:T(1,128)} %get-tuple-element.328), kind=kLoop, calls=%fused_computation.27 | loop fusion | flops 8388608 | bytes 67108864 | tf_op jit(solution)/shard_map/vmap()/stack | solution.py:75
  (511 shorter events, 149.9 us)
Async XLA Ops:
  4.2 10.7 %all-to-all-start.1 = ((s32[8,1,8]{2,1,0:T(1,128)}), s32[8,1,8]{2,1,0:T(1,128)S(1)}, u32[]{:S(2)}, u32[]{:S(2)}) async-start(s32[8,1,8]{2,1,0:T(1,128)} %bitcast.3), calls=%async_computation.1 | async-start | bytes 8192 | tf_op jit(solution)/shard_map/all_to_all | solution.py:90
  14.9 96.1 %all-to-all-start = ((f32[8,8,4,2,16,128]{5,4,3,2,1,0:T(8,128)}), f32[8,8,4,2,16,128]{5,4,3,2,1,0:T(8,128)}, u32[]{:S(2)}, u32[]{:S(2)}) async-start(f32[8,8,4,2,16,128]{5,4,3,2,1,0:T(8,128)} %bitcast.60), calls=%async_computation | async-start | bytes 8388608 | tf_op jit(solution)/shard_map/all_to_all | solution.py:89
  116.0 341.2 %all-to-all-start.2 = ((f32[64,4,2,16,128]{4,3,2,1,0:T(8,128)}), f32[64,4,2,16,128]{4,3,2,1,0:T(8,128)}, u32[]{:S(2)}, u32[]{:S(2)}) async-start(f32[64,4,2,16,128]{4,3,2,1,0:T(8,128)} %gather_fusion.2), calls=%async_computation.2 | async-start | bytes 8388608 | tf_op jit(solution)/shard_map/all_to_all | solution.py:102
  513.2 5.0 copy-start.2
  513.2 52.3 %all-to-all-start.3 = ((f32[16,4,64,2,128]{4,3,1,0,2:T(2,128)}), f32[16,4,64,2,128]{4,3,1,0,2:T(2,128)}, u32[]{:S(2)}, u32[]{:S(2)}) async-start(f32[16,4,64,2,128]{4,3,1,0,2:T(2,128)} %copy.30), calls=%async_computation.3 | async-start | bytes 8388608 | tf_op jit(solution)/shard_map/all_to_all | solution.py:109
  570.8 2.2 copy-start
  570.8 3.5 copy-start.1
where the time goes:
time: 653 us; the launch traced here: 644 us
  other arithmetic  232 us (36%)
  loops' own time  158 us (24%)
  waiting for transfers between devices  117 us (18%)
  local copies, waits for them, and re-layouts  95 us (15%)
  matrix products  21.5 us (3%)
  starting transfers between devices  21.4 us (3%)
    another operation x1, loops' own time, legendre_table(): lax.scan(advance, start_state, jnp.arange(degrees).astype(jnp.float32))  158 us
    all_to_all x1, waiting for transfers between devices, body(): lax.all_to_all(outgoing, 'sub', split_axis=0, concat_axis=0, tiled=True)  87.2 us
    dynamic_update_slice x64, other arithmetic, legendre_table(): lax.scan(advance, start_state, jnp.arange(degrees).astype(jnp.float32))  53.7 us
    lt x64, other arithmetic, advance(): degree < order_col  40.1 us
    eq x64, other arithmetic, advance(): degree == order_col + 1.0  39.7 us
    dynamic_slice x64, local copies, waits for them, and re-layouts, legendre_table(): lax.scan(advance, start_state, jnp.arange(degrees).astype(jnp.float32))  39.2 us
    sub x1, other arithmetic, shift_children(): real_part = wave_re * phase_cos - wave_im * phase_sin  36.9 us
    another operation x1, other arithmetic, shift_children(): return jnp.stack([real_part, imag_part], axis=-2)  32.8 us
  transfers between devices with their start and end apart: 4, of which 2 were waited for; matrix products, arithmetic and copies ran while one was open for 32% of the time, Pallas kernels for 0%

commit v1 on v0

v1 whole, which is shorter than its diff:
```python
import functools
import math

import jax
import jax.numpy as jnp
import numpy as np
from jax import lax
from jax.experimental import pallas as pl
from jax.experimental.pallas import tpu as pltpu
from jax.sharding import PartitionSpec as P

J = 64
K = 128
GROUP = 4


def legendre_constants(degrees, columns):
    q = np.abs(np.arange(columns) - degrees).astype(np.float64)
    log_norm = np.array(
        [
            0.5
            * (
                math.log((2 * v + 1) / (4 * math.pi))
                + math.lgamma(2 * v + 1)
                - v * math.log(4.0)
                - 2 * math.lgamma(v + 1)
            )
            for v in q
        ]
    )
    l = np.arange(degrees, dtype=np.float64)[:, None]
    numer = np.maximum(4 * l * l - 1, 1.0)
    denom = np.maximum(l * l - q[None] ** 2, 1.0)
    factor = np.sqrt(numer / denom)
    before = np.ones_like(factor)
    before[1:] = 1.0 / factor[:-1]
    return (
        log_norm.astype(np.float32)[None],
        q.astype(np.float32)[None],
        factor.astype(np.float32)[:, None, :],
        before.astype(np.float32)[:, None, :],
    )


def wave_matrix(degrees, columns, azimuths):
    turns = ((np.arange(columns)[:, None] - degrees) * np.arange(azimuths)[None, :]) % azimuths
    angle = 2.0 * np.pi * turns / azimuths
    cosine, sine = np.cos(angle), np.sin(angle)
    left = np.concatenate([cosine, -sine], axis=0)
    right = np.concatenate([-sine, -cosine], axis=0)
    return np.concatenate([left, right], axis=1).astype(np.float32)


def phase_tables(polar, azimuths):
    azimuth = 2.0 * jnp.pi * jnp.arange(azimuths).astype(jnp.float32) / azimuths
    octants = jnp.arange(8, dtype=jnp.int32)
    dir_x = jnp.sin(polar)[:, None] * jnp.cos(azimuth)[None, :]
    dir_y = jnp.sin(polar)[:, None] * jnp.sin(azimuth)[None, :]
    dir_z = jnp.cos(polar)[:, None] * jnp.ones_like(azimuth)[None, :]
    sign_x = (2 * (octants & 1) - 1).astype(jnp.float32)[:, None, None]
    sign_y = (2 * (octants >> 1 & 1) - 1).astype(jnp.float32)[:, None, None]
    sign_z = (2 * (octants >> 2 & 1) - 1).astype(jnp.float32)[:, None, None]
    phase = 5.5 * (sign_x * dir_x[None] + sign_y * dir_y[None] + sign_z * dir_z[None])
    return jnp.repeat(jnp.cos(phase), 2, axis=1), jnp.repeat(jnp.sin(phase), 2, axis=1)


def fill_table(tab, diag_ref, cos_ref, order_ref, factor_ref, before_ref):
    degrees = tab.shape[0]
    diag = diag_ref[...]
    cosines = cos_ref[...]
    order = jnp.broadcast_to(order_ref[...], diag.shape)
    next_value = jnp.sqrt(2.0 * order + 3.0) * cosines * diag

    def advance(degree, state):
        previous, before = state
        level = lax.convert_element_type(degree, jnp.float32)
        recur = factor_ref[degree] * (cosines * previous - before * before_ref[degree])
        value = jnp.where(level == order + 1.0, next_value, recur)
        value = jnp.where(level == order, diag, value)
        value = jnp.where(level < order, 0.0, value)
        tab[degree] = value
        return value, previous

    zeros = diag - diag
    lax.fori_loop(0, degrees, advance, (zeros, zeros))


def transform(source, child, *refs):
    coefs = refs[:GROUP]
    diag, cosines, order, factor, before, matrix, phase_cos, phase_sin, out, tab, upper, lower = refs[GROUP:]
    step = pl.program_id(0)

    @pl.when(step == 0)
    def _():
        fill_table(tab, diag, cosines, order, factor, before)

    parts, _, cases, _, depth, columns = coefs[0].shape
    width = tab.shape[1]
    rows = 2 * width
    for box in range(GROUP):
        coef = coefs[box]

        def add(part, totals):
            totals = list(totals)
            for inner in range(depth):
                weight = tab[part * depth + inner]
                for case in range(cases):
                    for half in range(2):
                        value = coef[part, 0, case, half, pl.ds(inner, 1), :]
                        slot = case * 2 + half
                        totals[slot] = totals[slot] + jnp.broadcast_to(value, (width, columns)) * weight
            return tuple(totals)

        zeros = tab[0] - tab[0]
        totals = lax.fori_loop(0, parts, add, (zeros,) * (2 * cases))
        for case in range(cases):
            base = (box * cases + case) * rows
            real, imag = totals[2 * case], totals[2 * case + 1]
            upper[pl.ds(base, width, 2), :] = real
            upper[pl.ds(base + 1, width, 2), :] = imag
            lower[pl.ds(base, width, 2), :] = imag
            lower[pl.ds(base + 1, width, 2), :] = -real
    both = jnp.concatenate([upper[...], lower[...]], axis=1)
    spread = jnp.dot(both, matrix[...], precision=lax.Precision.HIGHEST, preferred_element_type=jnp.float32)
    for box in range(GROUP):
        for place in range(8):
            octant = child[(step * GROUP + box) * 8 + place]
            turn_cos = phase_cos[octant]
            turn_sin = phase_sin[octant]
            for case in range(cases):
                base = (box * cases + case) * rows
                wave = spread[base : base + rows, :K]
                quarter = spread[base : base + rows, K:]
                out[box, case, place] = wave * turn_cos + quarter * turn_sin


def make_children(gathered, source, child_list, blk_index):
    parts, boxes, cases, _, depth, columns = gathered.shape
    degrees = parts * depth
    width = J // parts
    polar_all = jnp.pi * (jnp.arange(J).astype(jnp.float32) + 0.5) / J
    polar = lax.dynamic_slice_in_dim(polar_all, blk_index * width, width, 0)
    log_norm, order, factor, before = legendre_constants(degrees, columns)
    diag = jnp.exp(log_norm + order * jnp.log(jnp.sin(polar))[:, None])
    cosines = jnp.broadcast_to(jnp.cos(polar)[:, None], (width, columns))
    phase_cos, phase_sin = phase_tables(polar, K)
    matrix = jnp.asarray(wave_matrix(degrees, columns, K))

    def pick(offset):
        return pl.BlockSpec(
            (parts, 1, cases, 2, depth, columns),
            lambda i, source, child: (0, source[i * GROUP + offset], 0, 0, 0, 0),
        )

    whole = pl.BlockSpec(memory_space=pltpu.VMEM)
    rows = GROUP * cases * 2 * width
    out = pl.pallas_call(
        transform,
        grid_spec=pltpu.PrefetchScalarGridSpec(
            num_scalar_prefetch=2,
            grid=(boxes // GROUP,),
            in_specs=[pick(n) for n in range(GROUP)] + [whole] * 8,
            out_specs=pl.BlockSpec(
                (GROUP, cases, 8, 2 * width, K), lambda i, source, child: (i, 0, 0, 0, 0)
            ),
            scratch_shapes=[
                pltpu.VMEM((degrees, width, columns), jnp.float32),
                pltpu.VMEM((rows, columns), jnp.float32),
                pltpu.VMEM((rows, columns), jnp.float32),
            ],
        ),
        out_shape=jax.ShapeDtypeStruct((boxes, cases, 8, 2 * width, K), jnp.float32),
        compiler_params=pltpu.CompilerParams(vmem_limit_bytes=40 * 1024 * 1024),
        name="transform",
    )(
        source,
        child_list.reshape(-1),
        *([gathered] * GROUP),
        diag,
        cosines,
        jnp.asarray(order),
        jnp.asarray(factor),
        jnp.asarray(before),
        matrix,
        phase_cos,
        phase_sin,
    )
    return out.reshape(boxes, cases, 8, width, 2, K)


def body(coefficients, owner_slot, child_list):
    box_count = coefficients.shape[0]
    sub_count = lax.axis_size("sub")
    per_peer = box_count // sub_count
    targets = owner_slot // box_count
    positions = owner_slot % box_count
    send_order = jnp.argsort(targets, stable=True)
    outgoing = coefficients[send_order].reshape((sub_count, per_peer) + coefficients.shape[1:])
    placed = positions[send_order].reshape(sub_count, per_peer)
    arrived = lax.all_to_all(outgoing, "sub", split_axis=0, concat_axis=0, tiled=True)
    arrived_slots = lax.all_to_all(placed, "sub", split_axis=0, concat_axis=0, tiled=True)
    source = jnp.argsort(arrived_slots.reshape(-1)).astype(jnp.int32)
    gathered = lax.all_gather(arrived.reshape(coefficients.shape), "blk")
    return make_children(gathered, source, child_list, lax.axis_index("blk"))


def solution(mesh):
    placed = (P("sub", None, None, "blk", None), P("sub"), P("sub", None))
    return jax.shard_map(
        body,
        mesh=mesh,
        in_specs=placed,
        out_specs=P("sub", None, None, "blk", None, None),
        check_vma=False,
    )
```

time: 653 us -> 264 us (0.40); the launches traced: 644 us -> 263 us
  other arithmetic: 232 us -> 5.97 us
  loops' own time: 158 us -> 0 us
  blocking collectives: 0 us -> 96 us
  local copies, waits for them, and re-layouts: 95 us -> 7.56 us
  Pallas kernels: 0 us -> 37 us
  matrix products: 21.5 us -> 0 us
  waiting for transfers between devices: 117 us -> 96.7 us
  starting transfers between devices: 21.4 us -> 6.23 us
  between operations: 0.29 us -> 13.5 us
    another operation x1 -> x0, loops' own time: 158 us -> none  [legendre_table(): lax.scan(advance, start_state, jnp.arange(degrees).astype(jnp.float32))]
    all_to_all x3 -> x0, waiting for transfers between devices: 117 us -> none  [the longest x1 87.2 us: body(): lax.all_to_all(outgoing, 'sub', split_axis=0, concat_axis=0, tiled=True)]
    all_to_all x0 -> x1, blocking collectives: none -> 96 us  [body(): lax.all_to_all(outgoing, 'sub', split_axis=0, concat_axis=0, tiled=True)]
    all_gather x0 -> x1, waiting for transfers between devices: none -> 94.3 us  [body(): gathered = lax.all_gather(arrived.reshape(coefficients.shape), 'blk')]
    dynamic_update_slice x64 -> x0, other arithmetic: 53.7 us -> none  [legendre_table(): lax.scan(advance, start_state, jnp.arange(degrees).astype(jnp.float32))]
    lt x64 -> x0, other arithmetic: 40.1 us -> none  [advance(): degree < order_col]
    eq x64 -> x0, other arithmetic: 39.7 us -> none  [advance(): degree == order_col + 1.0]
    dynamic_slice x64 -> x0, local copies, waits for them, and re-layouts: 39.2 us -> none  [legendre_table(): lax.scan(advance, start_state, jnp.arange(degrees).astype(jnp.float32))]
  transfers between devices with their start and end apart: 4 -> 2, of which waited for: 2 -> 2; matrix products, arithmetic and copies ran while one was open for 32% -> 2% of each run, Pallas kernels for 0% -> 0%
where the time goes in v1:
time: 264 us; the launch traced here: 263 us
  waiting for transfers between devices  96.7 us (37%)
  blocking collectives  96 us (36%)
  Pallas kernels  37 us (14%)
  between operations  13.5 us (5%)
  local copies, waits for them, and re-layouts  7.56 us (3%)
  starting transfers between devices  6.23 us (2%)
  other arithmetic  5.97 us (2%)
    all_to_all x1, blocking collectives, body(): lax.all_to_all(outgoing, 'sub', split_axis=0, concat_axis=0, tiled=True)  96 us
    all_gather x1, waiting for transfers between devices, body(): gathered = lax.all_gather(arrived.reshape(coefficients.shape), 'blk')  94.3 us
    pallas_call x1, Pallas kernels, make_children(): pl.pallas_call(transform, grid_spec=pltpu.PrefetchScalarGridSpec(num_scal...  37 us
    all_to_all x1, starting transfers between devices, body(): lax.all_to_all(placed, 'sub', split_axis=0, concat_axis=0, tiled=True)  6.23 us
  transfers between devices with their start and end apart: 2, of which 2 were waited for; matrix products, arithmetic and copies ran while one was open for 2% of the time, Pallas kernels for 0%

profile of v1, /device:TPU:11, one launch (start us, length us, event | category | flops | bytes accessed | tf_op | source)
XLA Modules:
  0.0 262.9 jit_solution(4699817423577555198)
XLA Ops:
  6.5 0.0 all-gather.2.cloned.1.call-start
  6.5 0.7 and_select_fusion
  7.2 2.0 sort.34
  9.3 5.0 %gather_fusion.1 = f32[64,4,2,16,128]{4,3,2,1,0:T(8,128)} fusion(f32[64,4,2,16,128]{4,3,2,1,0:T(8,128)} %param.8, s32[1024]{0:T(1024)S(1)} %pad_clamp_fusion), kind=kCustom, calls=%fused_computation.1 | custom fusion | bytes 8388864 | tf_op jit(solution)/shard_map/gather | solution.py:198
  14.3 96.0 %all_to_all.14 = f32[8,8,4,2,16,128]{5,4,3,2,1,0:T(8,128)} all-to-all(f32[8,8,4,2,16,128]{5,4,3,2,1,0:T(8,128)} %bitcast.9), channel_id=1, replica_groups=mesh['sub'=8,'blk'=4] {'sub'}, dimensions={0} | all-to-all | bytes 8388608 | tf_op jit(solution)/shard_map/all_to_all | solution.py:200
  110.2 0.0 copy-start.5
  110.2 0.0 copy-start.6
  110.2 0.0 copy-start.4
  110.2 0.0 copy-start
  110.2 0.0 copy-start.1
  110.2 0.0 copy-start.2
  110.3 0.0 copy-start.3
  110.3 0.0 all-gather.2.cloned.1.call-update
  110.3 0.8 gather_fusion
  111.1 0.7 all_to_all.9
  111.8 6.2 %all-to-all-start = ((s32[8,1,8]{2,1,0:T(1,128)}), s32[8,1,8]{2,1,0:T(1,128)S(1)}, u32[]{:S(2)}, u32[]{:S(2)}) async-start(s32[8,1,8]{2,1,0:T(1,128)} %bitcast), calls=%async_computation | async-start | bytes 8192 | tf_op jit(solution)/shard_map/all_to_all | solution.py:201
  118.1 0.1 fusion.4
  118.2 0.1 broadcast_multiply_fusion.1
  118.2 0.3 fusion
  118.6 0.0 copy-done.5
  118.6 0.0 copy-done.6
  118.6 0.1 add_exponential_fusion.refs_4_
  118.7 0.0 copy-done.4
  118.7 0.1 copy.11
  118.8 0.1 reshape.108.child
  118.9 2.3 all-to-all-done
  121.2 0.5 broadcast.159
  121.7 0.7 reduce.3
  122.4 0.1 reshape.107
  122.4 2.0 sort.35
  124.5 94.3 %all-gather.2.cloned.1.call-done.refs_0_.refs_1_.refs_2_.refs_3_ = f32[4,64,4,2,16,128]{5,4,3,2,1,0:T(8,128)} async-done(((f32[1,64,4,2,16,128]{5,4,3,2,1,0:T(8,128)}), f32[4,64,4,2,16,128]{5,4,3,2,1,0:T(8,128)}) %all-gather.2.cloned.1.call-update) | async-done | bytes 16777232 | tf_op jit(solution)/shard_map/all_gather | solution.py:203
  218.8 0.1 broadcast_in_dim.9.refs_5_
  219.0 0.0 copy-done
  219.0 0.0 copy-done.1
  219.0 0.0 copy-done.2
  219.0 0.0 copy-done.3
  219.0 37.0 %transform.1 = f32[64,4,8,32,128]{4,3,2,1,0:T(8,128)} custom-call(s32[64]{0:T(128)S(1)} %get-tuple-element.8.source, s32[512]{0:T(512)S(1)} %reshape.108.child, f32[4,64,4,2,16,128]{5,4,3,2,1,0:T(8,128)} %all-gather.2.cloned.1.call-done.refs_0_.refs_1_.refs_2_.refs_3_, ...), custom_call_target="tpu_custom_call" | custom-call | tf_op jit(solution)/shard_map/transform/pallas_call | solution.py:157
  (10 shorter events, 0.2 us)
Async XLA Ops:
  6.5 212.3 %all-gather.2.cloned.1.call-start = ((), (), s32[]{:S(2)}) async-start(), calls=%async_computation.2 | async-start | bytes 20971520 | tf_op jit(solution)/shard_map/all_gather | solution.py:203
  110.2 8.4 %copy-start.5 = (f32[128]{0:T(128)S(1)}, f32[128]{0:T(128)}, u32[]{:S(2)}) copy-start(f32[128]{0:T(128)} %constant.72) | copy-start | bytes 1540
  110.2 8.4 %copy-start.6 = (f32[128]{0:T(128)S(1)}, f32[128]{0:T(128)}, u32[]{:S(2)}) copy-start(f32[128]{0:T(128)} %constant.71) | copy-start | bytes 1540
  110.2 8.5 %copy-start.4 = (s32[64,8]{0,1:T(8,128)S(1)}, s32[64,8]{0,1:T(8,128)}, u32[]{:S(2)}) copy-start(s32[64,8]{0,1:T(8,128)} %param.10) | copy-start | bytes 6148
  110.2 108.8 %copy-start = (f32[256,256]{1,0:T(8,128)S(1)}, f32[256,256]{1,0:T(8,128)}, u32[]{:S(2)}) copy-start(f32[256,256]{1,0:T(8,128)} %constant.68.clone.refs_9_) | copy-start | bytes 786436
  110.2 108.8 %copy-start.1 = (f32[64,1,128]{2,1,0:T(1,128)S(1)}, f32[64,1,128]{2,1,0:T(1,128)}, u32[]{:S(2)}) copy-start(f32[64,1,128]{2,1,0:T(1,128)} %constant.70.clone.refs_8_) | copy-start | bytes 98308
  110.2 108.8 %copy-start.2 = (f32[64,1,128]{2,1,0:T(1,128)S(1)}, f32[64,1,128]{2,1,0:T(1,128)}, u32[]{:S(2)}) copy-start(f32[64,1,128]{2,1,0:T(1,128)} %constant.69.clone.refs_7_) | copy-start | bytes 98308
  110.3 108.8 %copy-start.3 = (f32[1,128]{1,0:T(1,128)S(1)}, f32[1,128]{1,0:T(1,128)}, u32[]{:S(2)}) copy-start(f32[1,128]{1,0:T(1,128)} %constant.66.clone.refs_6_) | copy-start | bytes 1540
  111.8 9.4 %all-to-all-start = ((s32[8,1,8]{2,1,0:T(1,128)}), s32[8,1,8]{2,1,0:T(1,128)S(1)}, u32[]{:S(2)}, u32[]{:S(2)}) async-start(s32[8,1,8]{2,1,0:T(1,128)} %bitcast), calls=%async_computation | async-start | bytes 8192 | tf_op jit(solution)/shard_map/all_to_all | solution.py:201
Sparse Core Ops, SparseCore 0:
  110.4 108.3 all-gather.1

commit v2 on v1

--- a/solution.py
+++ b/solution.py
@@ -188,19 +188,202 @@
     return out.reshape(boxes, cases, 8, width, 2, K)
 
 
+def swapped(index, step, size):
+    total = 0
+    bit = 1
+    while bit < size:
+        total = total + ((index // bit + step // bit) % 2) * bit
+        bit *= 2
+    return total
+
+
+def exchange(
+    sub_count,
+    chips,
+    blocks,
+    slots,
+    gathered,
+    placed,
+    send_far,
+    recv_far,
+    send_near,
+    recv_near,
+    send_pair,
+    recv_pair,
+    send_slot,
+    recv_slot,
+    local,
+):
+    per_peer = blocks.shape[1]
+    steps = sub_count * per_peer
+    sub = lax.axis_index("sub")
+    blk = lax.axis_index("blk")
+    chip = blk // 2
+    core = blk % 2
+    sibling = chip * 2 + (1 - core)
+
+    def remote(source, target, send, recv, device):
+        return pltpu.make_async_remote_copy(
+            src_ref=source,
+            dst_ref=target,
+            send_sem=send,
+            recv_sem=recv,
+            device_id=device,
+            device_id_type=pl.DeviceIdType.MESH,
+        )
+
+    def far(step, box):
+        peer = swapped(sub, step, sub_count)
+        return remote(
+            blocks.at[peer, box],
+            gathered.at[blk, sub, box],
+            send_far.at[step, box],
+            recv_far.at[step, box],
+            (peer, blk),
+        )
+
+    def slot_copy(step):
+        peer = swapped(sub, step, sub_count)
+        return remote(slots.at[peer], placed.at[sub], send_slot.at[step], recv_slot.at[step], (peer, blk))
+
+    def held(hop):
+        return ((chip + chips - hop) % chips) * 2 + core
+
+    def near(hop, step, box, own):
+        source = swapped(sub, step, sub_count)
+        origin = blocks.at[sub, box] if own else gathered.at[blk, source, box]
+        return remote(
+            origin,
+            gathered.at[blk, source, box],
+            send_near.at[hop - 1, step, box],
+            recv_near.at[hop - 1, step, box],
+            (sub, ((chip + hop) % chips) * 2 + core),
+        )
+
+    def pair(hop, step, box, own=False):
+        source = swapped(sub, step, sub_count)
+        part = held(hop)
+        origin = blocks.at[sub, box] if own else gathered.at[part, source, box]
+        return remote(
+            origin,
+            gathered.at[part, source, box],
+            send_pair.at[hop, step, box],
+            recv_pair.at[hop, step, box],
+            (sub, sibling),
+        )
+
+    barrier = pltpu.get_barrier_semaphore()
+
+    def greet(device):
+        pl.semaphore_signal(barrier, inc=1, device_id=device, device_id_type=pl.DeviceIdType.MESH)
+
+    for step in range(1, sub_count):
+        greet((swapped(sub, step, sub_count), blk))
+    for hop in range(1, chips):
+        greet((sub, ((chip + hop) % chips) * 2 + core))
+    greet((sub, sibling))
+    pl.semaphore_wait(barrier, sub_count - 1 + chips)
+
+    order = [step for step in range(sub_count // 2, sub_count)] + list(range(1, sub_count // 2))
+    for step in order:
+        slot_copy(step).start()
+
+    @pl.loop(0, per_peer)
+    def _(box):
+        for step in order:
+            far(step, box).start()
+
+    keep_slot = pltpu.make_async_copy(slots.at[sub], placed.at[sub], local.at[0])
+    keep_slot.start()
+    keep_blocks = pltpu.make_async_copy(blocks.at[sub], gathered.at[blk, sub], local.at[1])
+    keep_blocks.start()
+
+    def relay(step, box):
+        for hop in range(1, chips):
+            near(hop, step, box, False).wait_recv()
+            pair(hop, step, box).start()
+
+    def arrive(step, box):
+        if step > 0:
+            far(step, box).wait_recv()
+        for hop in range(1, chips):
+            near(hop, step, box, step == 0).start()
+        pair(0, step, box, step == 0).start()
+
+    for step in range(sub_count):
+        arrive(step, 0)
+
+    @pl.loop(1, per_peer)
+    def _(box):
+        for step in range(sub_count):
+            arrive(step, box)
+            relay(step, box - 1)
+
+    for step in range(sub_count):
+        relay(step, per_peer - 1)
+
+    @pl.loop(0, per_peer)
+    def _(box):
+        for step in range(sub_count):
+            if step > 0:
+                far(step, box).wait_send()
+            for hop in range(1, chips):
+                near(hop, step, box, step == 0).wait_send()
+            for hop in range(chips):
+                pair(hop, step, box, step == 0 and hop == 0).wait()
+
+    for step in order:
+        slot_copy(step).wait()
+    keep_slot.wait()
+    keep_blocks.wait()
+
+
+def exchange_all(outgoing, slots, parts):
+    sub_count, per_peer, rows, columns = outgoing.shape
+    chips = parts // 2
+    dma = pltpu.SemaphoreType.DMA
+    anywhere = pl.BlockSpec(memory_space=pl.ANY)
+    vmem = pl.BlockSpec(memory_space=pltpu.VMEM)
+    hops = max(chips - 1, 1)
+    return pl.pallas_call(
+        functools.partial(exchange, sub_count, chips),
+        out_shape=(
+            jax.ShapeDtypeStruct((parts, sub_count, per_peer, rows, columns), jnp.float32),
+            jax.ShapeDtypeStruct(slots.shape, jnp.int32),
+        ),
+        in_specs=[anywhere, vmem],
+        out_specs=(anywhere, vmem),
+        scratch_shapes=[
+            dma((sub_count, per_peer)),
+            dma((sub_count, per_peer)),
+            dma((hops, sub_count, per_peer)),
+            dma((hops, sub_count, per_peer)),
+            dma((chips, sub_count, per_peer)),
+            dma((chips, sub_count, per_peer)),
+            dma((sub_count,)),
+            dma((sub_count,)),
+            dma((2,)),
+        ],
+        compiler_params=pltpu.CompilerParams(collective_id=0, has_side_effects=True),
+        name="exchange",
+    )(outgoing, slots)
+
+
 def body(coefficients, owner_slot, child_list):
-    box_count = coefficients.shape[0]
+    box_count, cases, _, depth, columns = coefficients.shape
     sub_count = lax.axis_size("sub")
+    parts = lax.axis_size("blk")
     per_peer = box_count // sub_count
     targets = owner_slot // box_count
     positions = owner_slot % box_count
     send_order = jnp.argsort(targets, stable=True)
-    outgoing = coefficients[send_order].reshape((sub_count, per_peer) + coefficients.shape[1:])
-    placed = positions[send_order].reshape(sub_count, per_peer)
-    arrived = lax.all_to_all(outgoing, "sub", split_axis=0, concat_axis=0, tiled=True)
-    arrived_slots = lax.all_to_all(placed, "sub", split_axis=0, concat_axis=0, tiled=True)
-    source = jnp.argsort(arrived_slots.reshape(-1)).astype(jnp.int32)
-    gathered = lax.all_gather(arrived.reshape(coefficients.shape), "blk")
+    flat = coefficients.reshape(box_count, cases * 2 * depth, columns)
+    outgoing = flat[send_order].reshape(sub_count, per_peer, cases * 2 * depth, columns)
+    slots = positions[send_order].reshape(sub_count, 1, per_peer)
+    slots = jnp.pad(slots, ((0, 0), (0, 0), (0, 128 - per_peer)))
+    gathered, placed = exchange_all(outgoing, slots, parts)
+    source = jnp.argsort(placed[:, 0, :per_peer].reshape(-1)).astype(jnp.int32)
+    gathered = gathered.reshape(parts, box_count, cases, 2, depth, columns)
     return make_children(gathered, source, child_list, lax.axis_index("blk"))
 
 

time: 264 us -> 181 us (0.69)
  Pallas kernels: 37 us -> 166 us
  waiting for transfers between devices: 96.7 us -> 0 us
  blocking collectives: 96 us -> 0 us
  between operations: 13.5 us -> 0.07 us
  starting transfers between devices: 6.23 us -> 0 us
    pallas_call x0 -> x1, Pallas kernels: none -> 130 us  [exchange_all(): pl.pallas_call(functools.partial(exchange, sub_count, chips), out_shape=(...]
    all_to_all x1 -> x0, blocking collectives: 96 us -> none  [body(): lax.all_to_all(outgoing, 'sub', split_axis=0, concat_axis=0, tiled=True)]
    all_gather x1 -> x0, waiting for transfers between devices: 94.3 us -> none  [body(): gathered = lax.all_gather(arrived.reshape(coefficients.shape), 'blk')]
    all_to_all x1 -> x0, starting transfers between devices: 6.23 us -> none  [body(): lax.all_to_all(placed, 'sub', split_axis=0, concat_axis=0, tiled=True)]
  transfers between devices with their start and end apart: 2 -> 0, of which waited for: 2 -> 0; matrix products, arithmetic and copies ran while one was open for 2% -> 0% of each run, Pallas kernels for 0% -> 0%
where the time goes in v2:
time: 181 us
  Pallas kernels  166 us (92%)
  local copies, waits for them, and re-layouts  8.42 us (5%)
  other arithmetic  5.94 us (3%)
    pallas_call x1, Pallas kernels, exchange_all(): pl.pallas_call(functools.partial(exchange, sub_count, chips), out_shape=(...  130 us
    pallas_call x1, Pallas kernels, make_children(): pl.pallas_call(transform, grid_spec=pltpu.PrefetchScalarGridSpec(num_scal...  36.9 us
    gather x1, local copies, waits for them, and re-layouts, body(): flat[send_order].reshape(sub_count, per_peer, cases * 2 * depth, columns)  5.02 us

profile of v2, /device:TPU:11, one launch (start us, length us, event | category | flops | bytes accessed | tf_op | source)
XLA Modules:
  0.0 180.9 jit_solution(9581843835105509197)
XLA Ops:
  0.1 0.1 fusion.4
  0.2 0.7 and_select_fusion
  0.9 2.0 %sort.34 = (s32[64]{0:T(128)}, s32[64]{0:T(128)S(1)}) sort(s32[64]{0:T(128)S(1)} %get-tuple-element.21, s32[64]{0:T(128)S(1)} %iota.33), dimensions={0}, to_apply=%region_0.1 | sort | flops 384 | bytes 1024 | tf_op jit(solution)/shard_map/jit(argsort)/sort | solution.py:379
  3.0 0.8 gather_fusion.1
  3.7 0.1 reshape.110
  3.8 0.6 pad.4.slots
  4.4 0.1 broadcast_in_dim.9.refs_5_
  4.5 0.7 broadcast_multiply_fusion.1
  5.2 0.8 copy.11
  6.0 0.1 reshape.111.child
  6.1 0.3 fusion
  6.6 5.0 %gather_fusion = f32[64,128,128]{2,1,0:T(8,128)} fusion(f32[64,128,128]{2,1,0:T(8,128)} %bitcast.14, s32[1024]{0:T(1024)S(1)} %pad_clamp_fusion), kind=kCustom, calls=%fused_computation | custom fusion | bytes 8388864 | tf_op jit(solution)/shard_map/gather | solution.py:381
  11.6 0.0 copy-start
  11.6 0.0 copy-start.1
  11.6 0.0 copy-start.2
  11.6 0.0 copy-start.3
  11.6 129.6 %exchange.1 = (f32[4,8,8,128,128]{4,3,2,1,0:T(8,128)}, s32[8,1,128]{2,1,0:T(1,128)}) custom-call(f32[8,8,128,128]{3,2,1,0:T(8,128)} %bitcast.13, s32[8,1,128]{2,1,0:T(1,128)} %pad.4.slots), custom_call_target="tpu_custom_call" | custom-call | tf_op jit(solution)/shard_map/exchange/pallas_call | solution.py:348
  141.2 0.7 slice_reduce_fusion
  141.9 0.1 reshape_squeeze.3
  142.0 2.0 %sort.35 = (s32[64]{0:T(128)}, s32[64]{0:T(128)S(1)}) sort(s32[64]{0:T(128)S(1)} %reshape_squeeze.3, s32[64]{0:T(128)S(1)} %iota.34), dimensions={0}, to_apply=%region_1.2 | sort | flops 384 | bytes 1024 | tf_op jit(solution)/shard_map/jit(argsort)/sort | solution.py:385
  144.0 0.0 copy-done
  144.0 0.0 copy-done.1
  144.0 0.0 copy-done.2
  144.0 0.0 copy-done.3
  144.0 36.9 %transform.1 = f32[64,4,8,32,128]{4,3,2,1,0:T(8,128)} custom-call(s32[64]{0:T(128)S(1)} %get-tuple-element.11.source, s32[512]{0:T(512)S(1)} %reshape.111.child, f32[4,64,4,2,16,128]{5,4,3,2,1,0:T(8,128)} %bitcast.9, f32[4,64,4,2,16,128]{5,4,3,2,1,0:T(8,128)} %bitcast.10, f32[4,64,4,2,16,128]{5,4,3,2,1,0:T(8,128)} %bitcast.11, ...), custom_call_target="tpu_custom_call" | custom-call | tf_op jit(solution)/shard_map/transform/pallas_call | solution.py:157
  (11 shorter events, 0.2 us)
Async XLA Ops:
  11.6 132.4 %copy-start = (f32[256,256]{1,0:T(8,128)S(1)}, f32[256,256]{1,0:T(8,128)}, u32[]{:S(2)}) copy-start(f32[256,256]{1,0:T(8,128)} %constant.68.clone.refs_9_) | copy-start | bytes 786436
  11.6 132.4 %copy-start.1 = (f32[64,1,128]{2,1,0:T(1,128)S(1)}, f32[64,1,128]{2,1,0:T(1,128)}, u32[]{:S(2)}) copy-start(f32[64,1,128]{2,1,0:T(1,128)} %constant.70.clone.refs_8_) | copy-start | bytes 98308
  11.6 132.4 %copy-start.2 = (f32[64,1,128]{2,1,0:T(1,128)S(1)}, f32[64,1,128]{2,1,0:T(1,128)}, u32[]{:S(2)}) copy-start(f32[64,1,128]{2,1,0:T(1,128)} %constant.69.clone.refs_7_) | copy-start | bytes 98308
  11.6 132.4 %copy-start.3 = (f32[1,128]{1,0:T(1,128)S(1)}, f32[1,128]{1,0:T(1,128)}, u32[]{:S(2)}) copy-start(f32[1,128]{1,0:T(1,128)} %constant.66.clone.refs_6_) | copy-start | bytes 1540

commit v3 on v2

--- a/solution.py
+++ b/solution.py
@@ -86,36 +86,16 @@
 
 
 def transform(source, child, *refs):
-    coefs = refs[:GROUP]
-    diag, cosines, order, factor, before, matrix, phase_cos, phase_sin, out, tab, upper, lower = refs[GROUP:]
+    cycles = refs[:GROUP]
+    matrix, phase_cos, phase_sin, out, upper, lower = refs[GROUP:]
     step = pl.program_id(0)
-
-    @pl.when(step == 0)
-    def _():
-        fill_table(tab, diag, cosines, order, factor, before)
-
-    parts, _, cases, _, depth, columns = coefs[0].shape
-    width = tab.shape[1]
+    _, lines, width, _ = cycles[0].shape
+    cases = lines // 2
     rows = 2 * width
     for box in range(GROUP):
-        coef = coefs[box]
-
-        def add(part, totals):
-            totals = list(totals)
-            for inner in range(depth):
-                weight = tab[part * depth + inner]
-                for case in range(cases):
-                    for half in range(2):
-                        value = coef[part, 0, case, half, pl.ds(inner, 1), :]
-                        slot = case * 2 + half
-                        totals[slot] = totals[slot] + jnp.broadcast_to(value, (width, columns)) * weight
-            return tuple(totals)
-
-        zeros = tab[0] - tab[0]
-        totals = lax.fori_loop(0, parts, add, (zeros,) * (2 * cases))
         for case in range(cases):
             base = (box * cases + case) * rows
-            real, imag = totals[2 * case], totals[2 * case + 1]
+            real, imag = cycles[box][0, 2 * case], cycles[box][0, 2 * case + 1]
             upper[pl.ds(base, width, 2), :] = real
             upper[pl.ds(base + 1, width, 2), :] = imag
             lower[pl.ds(base, width, 2), :] = imag
@@ -134,22 +114,22 @@
                 out[box, case, place] = wave * turn_cos + quarter * turn_sin
 
 
-def make_children(gathered, source, child_list, blk_index):
-    parts, boxes, cases, _, depth, columns = gathered.shape
-    degrees = parts * depth
+def own_polar(parts, blk_index):
     width = J // parts
     polar_all = jnp.pi * (jnp.arange(J).astype(jnp.float32) + 0.5) / J
-    polar = lax.dynamic_slice_in_dim(polar_all, blk_index * width, width, 0)
-    log_norm, order, factor, before = legendre_constants(degrees, columns)
-    diag = jnp.exp(log_norm + order * jnp.log(jnp.sin(polar))[:, None])
-    cosines = jnp.broadcast_to(jnp.cos(polar)[:, None], (width, columns))
-    phase_cos, phase_sin = phase_tables(polar, K)
-    matrix = jnp.asarray(wave_matrix(degrees, columns, K))
+    return lax.dynamic_slice_in_dim(polar_all, blk_index * width, width, 0)
+
+
+def make_children(cycles, source, child_list, parts, lines, blk_index):
+    boxes, _, width, columns = cycles.shape
+    cases = lines // 2
+    phase_cos, phase_sin = phase_tables(own_polar(parts, blk_index), K)
+    matrix = jnp.asarray(wave_matrix(columns // 2, columns, K))
 
     def pick(offset):
         return pl.BlockSpec(
-            (parts, 1, cases, 2, depth, columns),
-            lambda i, source, child: (0, source[i * GROUP + offset], 0, 0, 0, 0),
+            (1, lines, width, columns),
+            lambda i, source, child: (source[i * GROUP + offset], 0, 0, 0),
         )
 
     whole = pl.BlockSpec(memory_space=pltpu.VMEM)
@@ -159,12 +139,11 @@
         grid_spec=pltpu.PrefetchScalarGridSpec(
             num_scalar_prefetch=2,
             grid=(boxes // GROUP,),
-            in_specs=[pick(n) for n in range(GROUP)] + [whole] * 8,
+            in_specs=[pick(n) for n in range(GROUP)] + [whole] * 3,
             out_specs=pl.BlockSpec(
                 (GROUP, cases, 8, 2 * width, K), lambda i, source, child: (i, 0, 0, 0, 0)
             ),
             scratch_shapes=[
-                pltpu.VMEM((degrees, width, columns), jnp.float32),
                 pltpu.VMEM((rows, columns), jnp.float32),
                 pltpu.VMEM((rows, columns), jnp.float32),
             ],
@@ -172,19 +151,7 @@
         out_shape=jax.ShapeDtypeStruct((boxes, cases, 8, 2 * width, K), jnp.float32),
         compiler_params=pltpu.CompilerParams(vmem_limit_bytes=40 * 1024 * 1024),
         name="transform",
-    )(
-        source,
-        child_list.reshape(-1),
-        *([gathered] * GROUP),
-        diag,
-        cosines,
-        jnp.asarray(order),
-        jnp.asarray(factor),
-        jnp.asarray(before),
-        matrix,
-        phase_cos,
-        phase_sin,
-    )
+    )(source, child_list.reshape(-1), *([cycles] * GROUP), matrix, phase_cos, phase_sin)
     return out.reshape(boxes, cases, 8, width, 2, K)
 
 
@@ -202,8 +169,15 @@
     chips,
     blocks,
     slots,
+    diag,
+    cosines,
+    orders,
+    factor,
+    before,
+    cycles,
+    placed,
     gathered,
-    placed,
+    tab,
     send_far,
     recv_far,
     send_near,
@@ -284,9 +258,14 @@
     greet((sub, sibling))
     pl.semaphore_wait(barrier, sub_count - 1 + chips)
 
-    order = [step for step in range(sub_count // 2, sub_count)] + list(range(1, sub_count // 2))
-    for step in order:
+    order = list(range(sub_count // 2, sub_count)) + list(range(2, sub_count // 2))
+    everyone = [1] + order
+    for step in everyone:
         slot_copy(step).start()
+
+    @pl.loop(0, per_peer)
+    def _(box):
+        far(1, box).start()
 
     @pl.loop(0, per_peer)
     def _(box):
@@ -297,6 +276,26 @@
     keep_slot.start()
     keep_blocks = pltpu.make_async_copy(blocks.at[sub], gathered.at[blk, sub], local.at[1])
     keep_blocks.start()
+    fill_table(tab, diag, cosines, orders, factor, before)
+
+    parts, _, _, rows, columns = gathered.shape
+    degrees, width, _ = tab.shape
+    depth = degrees // parts
+    lines = rows // depth
+
+    def finish(step, box):
+        source = swapped(sub, step, sub_count)
+        for hop in range(chips):
+            pair(hop, step, box, step == 0 and hop == 0).wait_recv()
+
+        def add(part, total):
+            for inner in range(depth):
+                value = gathered[part, source, box, pl.ds(inner, lines, depth), :]
+                total = total + value[:, None, :] * tab[part * depth + inner][None]
+            return total
+
+        zeros = jnp.broadcast_to((tab[0] - tab[0])[None], (lines, width, columns))
+        cycles[source, box] = lax.fori_loop(0, parts, add, zeros)
 
     def relay(step, box):
         for hop in range(1, chips):
@@ -310,17 +309,41 @@
             near(hop, step, box, step == 0).start()
         pair(0, step, box, step == 0).start()
 
-    for step in range(sub_count):
+    @pl.loop(0, per_peer)
+    def _(box):
+        arrive(0, box)
+
+    @pl.loop(0, per_peer)
+    def _(box):
+        arrive(1, box)
+        relay(0, box)
+
+    keep_blocks.wait()
+    for step in order:
         arrive(step, 0)
+    relay(1, 0)
+    finish(0, 0)
 
     @pl.loop(1, per_peer)
     def _(box):
-        for step in range(sub_count):
+        for step in order:
             arrive(step, box)
             relay(step, box - 1)
-
-    for step in range(sub_count):
+        relay(1, box)
+        finish(0, box)
+        finish(1, box - 1)
+
+        @pl.when(box > 1)
+        def _():
+            for step in order:
+                finish(step, box - 2)
+
+    for step in order:
         relay(step, per_peer - 1)
+    finish(1, per_peer - 1)
+    for back in (2, 1):
+        for step in order:
+            finish(step, per_peer - back)
 
     @pl.loop(0, per_peer)
     def _(box):
@@ -330,17 +353,23 @@
             for hop in range(1, chips):
                 near(hop, step, box, step == 0).wait_send()
             for hop in range(chips):
-                pair(hop, step, box, step == 0 and hop == 0).wait()
-
-    for step in order:
+                pair(hop, step, box, step == 0 and hop == 0).wait_send()
+
+    for step in everyone:
         slot_copy(step).wait()
     keep_slot.wait()
-    keep_blocks.wait()
-
-
-def exchange_all(outgoing, slots, parts):
+
+
+def exchange_all(outgoing, slots, parts, depth, blk_index):
     sub_count, per_peer, rows, columns = outgoing.shape
     chips = parts // 2
+    degrees = parts * depth
+    width = J // parts
+    lines = rows // depth
+    polar = own_polar(parts, blk_index)
+    log_norm, order, factor, before = legendre_constants(degrees, columns)
+    diag = jnp.exp(log_norm + order * jnp.log(jnp.sin(polar))[:, None])
+    cosines = jnp.broadcast_to(jnp.cos(polar)[:, None], (width, columns))
     dma = pltpu.SemaphoreType.DMA
     anywhere = pl.BlockSpec(memory_space=pl.ANY)
     vmem = pl.BlockSpec(memory_space=pltpu.VMEM)
@@ -348,12 +377,14 @@
     return pl.pallas_call(
         functools.partial(exchange, sub_count, chips),
         out_shape=(
-            jax.ShapeDtypeStruct((parts, sub_count, per_peer, rows, columns), jnp.float32),
+            jax.ShapeDtypeStruct((sub_count, per_peer, lines, width, columns), jnp.float32),
             jax.ShapeDtypeStruct(slots.shape, jnp.int32),
         ),
-        in_specs=[anywhere, vmem],
-        out_specs=(anywhere, vmem),
+        in_specs=[anywhere] + [vmem] * 6,
+        out_specs=(vmem, vmem),
         scratch_shapes=[
+            pltpu.VMEM((parts, sub_count, per_peer, rows, columns), jnp.float32),
+            pltpu.VMEM((degrees, width, columns), jnp.float32),
             dma((sub_count, per_peer)),
             dma((sub_count, per_peer)),
             dma((hops, sub_count, per_peer)),
@@ -364,9 +395,19 @@
             dma((sub_count,)),
             dma((2,)),
         ],
-        compiler_params=pltpu.CompilerParams(collective_id=0, has_side_effects=True),
+        compiler_params=pltpu.CompilerParams(
+            collective_id=0, has_side_effects=True, vmem_limit_bytes=40 * 1024 * 1024
+        ),
         name="exchange",
-    )(outgoing, slots)
+    )(
+        outgoing,
+        slots,
+        diag,
+        cosines,
+        jnp.asarray(order),
+        jnp.asarray(factor),
+        jnp.asarray(before),
+    )
 
 
 def body(coefficients, owner_slot, child_list):
@@ -381,10 +422,11 @@
     outgoing = flat[send_order].reshape(sub_count, per_peer, cases * 2 * depth, columns)
     slots = positions[send_order].reshape(sub_count, 1, per_peer)
     slots = jnp.pad(slots, ((0, 0), (0, 0), (0, 128 - per_peer)))
-    gathered, placed = exchange_all(outgoing, slots, parts)
+    blk_index = lax.axis_index("blk")
+    cycles, placed = exchange_all(outgoing, slots, parts, depth, blk_index)
     source = jnp.argsort(placed[:, 0, :per_peer].reshape(-1)).astype(jnp.int32)
-    gathered = gathered.reshape(parts, box_count, cases, 2, depth, columns)
-    return make_children(gathered, source, child_list, lax.axis_index("blk"))
+    cycles = cycles.reshape((box_count,) + cycles.shape[2:])
+    return make_children(cycles, source, child_list, parts, 2 * cases, blk_index)
 
 
 def solution(mesh):

time: 181 us -> 163 us (0.901)
  Pallas kernels: 166 us -> 142 us
  local copies, waits for them, and re-layouts: 8.42 us -> 13.5 us
    pallas_call x1, Pallas kernels: 36.9 us -> 18.6 us  [make_children(): pl.pallas_call(transform, grid_spec=pltpu.PrefetchScalarGridSpec(num_scal...]
    unnamed x9 -> x15, local copies, waits for them, and re-layouts: 0.79 us -> 7.18 us
    pallas_call x1, Pallas kernels: 130 us -> 124 us  [exchange_all(): pl.pallas_call(functools.partial(exchange, sub_count, chips), out_shape=(...]
where the time goes in v3:
time: 163 us; the launch traced here: 162 us
  Pallas kernels  142 us (87%)
  local copies, waits for them, and re-layouts  13.5 us (8%)
  other arithmetic  6.02 us (4%)
    pallas_call x1, Pallas kernels, exchange_all(): pl.pallas_call(functools.partial(exchange, sub_count, chips), out_shape=(...  124 us
    pallas_call x1, Pallas kernels, make_children(): pl.pallas_call(transform, grid_spec=pltpu.PrefetchScalarGridSpec(num_scal...  18.6 us
    unnamed x15, local copies, waits for them, and re-layouts  7.18 us
    gather x1, local copies, waits for them, and re-layouts, body(): flat[send_order].reshape(sub_count, per_peer, cases * 2 * depth, columns)  5.03 us

profile of v3, /device:TPU:11, one launch (start us, length us, event | category | flops | bytes accessed | tf_op | source)
XLA Modules:
  0.0 162.0 jit_solution(2034879042965920594)
XLA Ops:
  0.1 0.1 fusion.4
  0.2 0.7 and_select_fusion
  0.9 2.0 %sort.34 = (s32[64]{0:T(128)}, s32[64]{0:T(128)S(1)}) sort(s32[64]{0:T(128)S(1)} %get-tuple-element.21, s32[64]{0:T(128)S(1)} %iota.34), dimensions={0}, to_apply=%region_0.1 | sort | flops 384 | bytes 1024 | tf_op jit(solution)/shard_map/jit(argsort)/sort | solution.py:420
  3.0 0.8 gather_fusion.1
  3.7 0.1 reshape.110
  3.8 0.1 broadcast_in_dim.9.cosines
  3.9 0.7 broadcast_multiply_fusion.1
  4.7 0.8 copy.11
  5.4 0.1 reshape.111.child
  5.5 0.3 fusion
  6.0 0.0 copy-start.4
  6.0 0.0 copy-start.5
  6.0 0.0 copy-start.6
  6.0 5.0 %gather_fusion = f32[64,128,128]{2,1,0:T(8,128)} fusion(f32[64,128,128]{2,1,0:T(8,128)} %bitcast.14, s32[1024]{0:T(1024)S(1)} %pad_clamp_fusion), kind=kCustom, calls=%fused_computation | custom fusion | bytes 8388864 | tf_op jit(solution)/shard_map/gather | solution.py:422
  11.0 0.0 copy-done.4
  11.0 0.0 copy-done.5
  11.0 0.0 copy-done.6
  11.1 0.0 copy-start.2
  11.1 2.2 %copy-done.2 = f32[64,128,128]{2,1,0:T(8,128)S(1)} copy-done((f32[64,128,128]{2,1,0:T(8,128)S(1)}, f32[64,128,128]{2,1,0:T(8,128)}, u32[]{:S(2)}) %copy-start.2) | copy-done | bytes 4194328
  13.2 0.0 copy-start.3
  13.2 123.7 %exchange.1 = (f32[8,8,8,16,128]{4,3,2,1,0:T(8,128)S(1)}, s32[8,1,128]{2,1,0:T(1,128)S(1)}) custom-call(f32[8,8,128,128]{3,2,1,0:T(8,128)S(1)} %bitcast.11, s32[8,1,128]{2,1,0:T(1,128)S(1)} %pad.4.slots, f32[16,128]{1,0:T(8,128)S(1)} %get-tuple-element.22.diag, f32[16,128]{1,0:T(8,128)S(1)} %broadcast_in_dim.9.cosines, f32[1,128]{1,0:T(1,128)S(1)} %copy-done.6, ...), custom_call_target="tpu_custom_call" | custom-call | tf_op jit(solution)/shard_map/exchange/pallas_call | solution.py:377
  137.0 0.0 copy-start
  137.0 2.0 %copy-done = f32[8,8,8,16,128]{4,3,2,1,0:T(8,128)} copy-done((f32[8,8,8,16,128]{4,3,2,1,0:T(8,128)}, f32[8,8,8,16,128]{4,3,2,1,0:T(8,128)S(1)}, u32[]{:S(2)}) %copy-start) | copy-done | bytes 4194328
  139.0 0.1 reshape_squeeze.3
  139.1 2.1 %sort.35 = (s32[64]{0:T(128)}, s32[64]{0:T(128)S(1)}) sort(s32[64]{0:T(128)S(1)} %reshape_squeeze.3, s32[64]{0:T(128)S(1)} %iota.36), dimensions={0}, to_apply=%region_1.2 | sort | flops 384 | bytes 1024 | tf_op jit(solution)/shard_map/jit(argsort)/sort | solution.py:427
  141.2 0.0 copy-done.3
  141.2 0.0 copy-start.1
  141.2 2.2 %copy-done.1 = f32[8,8,8,16,128]{4,3,2,1,0:T(8,128)S(1)} copy-done((f32[8,8,8,16,128]{4,3,2,1,0:T(8,128)S(1)}, f32[8,8,8,16,128]{4,3,2,1,0:T(8,128)}, u32[]{:S(2)}) %copy-start.1) | copy-done | bytes 4194328
  143.4 18.6 %transform.1 = f32[64,4,8,32,128]{4,3,2,1,0:T(8,128)} custom-call(s32[64]{0:T(128)S(1)} %get-tuple-element.11.source, s32[512]{0:T(512)S(1)} %reshape.111.child, f32[64,8,16,128]{3,2,1,0:T(8,128)S(1)} %bitcast.7, f32[64,8,16,128]{3,2,1,0:T(8,128)S(1)} %bitcast.8, f32[64,8,16,128]{3,2,1,0:T(8,128)S(1)} %bitcast.9, f32[64,8,16,128]{3,2,1,0:T(8,128)S(1)} %bitcast.10, ...), custom_call_target="tpu_custom_call" | custom-call | tf_op jit(solution)/shard_map/transform/pallas_call | solution.py:137
  (13 shorter events, 0.2 us)
Async XLA Ops:
  6.0 5.1 %copy-start.4 = (f32[64,1,128]{2,1,0:T(1,128)S(1)}, f32[64,1,128]{2,1,0:T(1,128)}, u32[]{:S(2)}) copy-start(f32[64,1,128]{2,1,0:T(1,128)} %constant.69.clone.before) | copy-start | bytes 98308
  6.0 5.1 %copy-start.5 = (f32[64,1,128]{2,1,0:T(1,128)S(1)}, f32[64,1,128]{2,1,0:T(1,128)}, u32[]{:S(2)}) copy-start(f32[64,1,128]{2,1,0:T(1,128)} %constant.68.clone.factor) | copy-start | bytes 98308
  6.0 5.0 %copy-start.6 = (f32[1,128]{1,0:T(1,128)S(1)}, f32[1,128]{1,0:T(1,128)}, u32[]{:S(2)}) copy-start(f32[1,128]{1,0:T(1,128)} %constant.66.clone.orders) | copy-start | bytes 1540
  11.1 2.2 %copy-start.2 = (f32[64,128,128]{2,1,0:T(8,128)S(1)}, f32[64,128,128]{2,1,0:T(8,128)}, u32[]{:S(2)}) copy-start(f32[64,128,128]{2,1,0:T(8,128)} %gather_fusion) | copy-start | bytes 12582916
  13.2 128.0 %copy-start.3 = (f32[256,256]{1,0:T(8,128)S(1)}, f32[256,256]{1,0:T(8,128)}, u32[]{:S(2)}) copy-start(f32[256,256]{1,0:T(8,128)} %constant.70.clone.refs_4_) | copy-start | bytes 786436
  137.0 2.0 %copy-start = (f32[8,8,8,16,128]{4,3,2,1,0:T(8,128)}, f32[8,8,8,16,128]{4,3,2,1,0:T(8,128)S(1)}, u32[]{:S(2)}) copy-start(f32[8,8,8,16,128]{4,3,2,1,0:T(8,128)S(1)} %get-tuple-element.12) | copy-start | bytes 12582916
  141.2 2.2 %copy-start.1 = (f32[8,8,8,16,128]{4,3,2,1,0:T(8,128)S(1)}, f32[8,8,8,16,128]{4,3,2,1,0:T(8,128)}, u32[]{:S(2)}) copy-start(f32[8,8,8,16,128]{4,3,2,1,0:T(8,128)} %copy-done) | copy-start | bytes 12582916

commit v4 on v3

--- a/solution.py
+++ b/solution.py
@@ -258,45 +258,6 @@
     greet((sub, sibling))
     pl.semaphore_wait(barrier, sub_count - 1 + chips)
 
-    order = list(range(sub_count // 2, sub_count)) + list(range(2, sub_count // 2))
-    everyone = [1] + order
-    for step in everyone:
-        slot_copy(step).start()
-
-    @pl.loop(0, per_peer)
-    def _(box):
-        far(1, box).start()
-
-    @pl.loop(0, per_peer)
-    def _(box):
-        for step in order:
-            far(step, box).start()
-
-    keep_slot = pltpu.make_async_copy(slots.at[sub], placed.at[sub], local.at[0])
-    keep_slot.start()
-    keep_blocks = pltpu.make_async_copy(blocks.at[sub], gathered.at[blk, sub], local.at[1])
-    keep_blocks.start()
-    fill_table(tab, diag, cosines, orders, factor, before)
-
-    parts, _, _, rows, columns = gathered.shape
-    degrees, width, _ = tab.shape
-    depth = degrees // parts
-    lines = rows // depth
-
-    def finish(step, box):
-        source = swapped(sub, step, sub_count)
-        for hop in range(chips):
-            pair(hop, step, box, step == 0 and hop == 0).wait_recv()
-
-        def add(part, total):
-            for inner in range(depth):
-                value = gathered[part, source, box, pl.ds(inner, lines, depth), :]
-                total = total + value[:, None, :] * tab[part * depth + inner][None]
-            return total
-
-        zeros = jnp.broadcast_to((tab[0] - tab[0])[None], (lines, width, columns))
-        cycles[source, box] = lax.fori_loop(0, parts, add, zeros)
-
     def relay(step, box):
         for hop in range(1, chips):
             near(hop, step, box, False).wait_recv()
@@ -309,9 +270,45 @@
             near(hop, step, box, step == 0).start()
         pair(0, step, box, step == 0).start()
 
+    order = list(range(sub_count // 2, sub_count)) + list(range(2, sub_count // 2))
+    everyone = [1] + order
+    for step in everyone:
+        slot_copy(step).start()
+
     @pl.loop(0, per_peer)
     def _(box):
         arrive(0, box)
+        far(1, box).start()
+
+        @pl.when(box < 2)
+        def _():
+            for step in order:
+                far(step, box).start()
+
+    keep_slot = pltpu.make_async_copy(slots.at[sub], placed.at[sub], local.at[0])
+    keep_slot.start()
+    keep_blocks = pltpu.make_async_copy(blocks.at[sub], gathered.at[blk, sub], local.at[1])
+    keep_blocks.start()
+    fill_table(tab, diag, cosines, orders, factor, before)
+
+    parts, _, _, rows, columns = gathered.shape
+    degrees, width, _ = tab.shape
+    depth = degrees // parts
+    lines = rows // depth
+
+    def finish(step, box):
+        source = swapped(sub, step, sub_count)
+        for hop in range(chips):
+            pair(hop, step, box, step == 0 and hop == 0).wait_recv()
+
+        def add(part, total):
+            for inner in range(depth):
+                value = gathered[part, source, box, pl.ds(inner, lines, depth), :]
+                total = total + value[:, None, :] * tab[part * depth + inner][None]
+            return total
+
+        zeros = jnp.broadcast_to((tab[0] - tab[0])[None], (lines, width, columns))
+        cycles[source, box] = lax.fori_loop(0, parts, add, zeros)
 
     @pl.loop(0, per_peer)
     def _(box):
@@ -326,6 +323,11 @@
 
     @pl.loop(1, per_peer)
     def _(box):
+        @pl.when(box + 1 < per_peer)
+        def _():
+            for step in order:
+                far(step, box + 1).start()
+
         for step in order:
             arrive(step, box)
             relay(step, box - 1)

time: 163 us -> 155 us (0.951)
  Pallas kernels: 142 us -> 134 us
    pallas_call x1, Pallas kernels: 124 us -> 116 us  [exchange_all(): pl.pallas_call(functools.partial(exchange, sub_count, chips), out_shape=(...]
where the time goes in v4:
time: 155 us; the launch traced here: 154 us
  Pallas kernels  134 us (86%)
  local copies, waits for them, and re-layouts  13.5 us (9%)
  other arithmetic  6.02 us (4%)
    pallas_call x1, Pallas kernels, exchange_all(): pl.pallas_call(functools.partial(exchange, sub_count, chips), out_shape=(...  116 us
    pallas_call x1, Pallas kernels, make_children(): pl.pallas_call(transform, grid_spec=pltpu.PrefetchScalarGridSpec(num_scal...  18.6 us
    unnamed x15, local copies, waits for them, and re-layouts  7.18 us
    gather x1, local copies, waits for them, and re-layouts, body(): flat[send_order].reshape(sub_count, per_peer, cases * 2 * depth, columns)  5.03 us

profile of v4, /device:TPU:11, one launch (start us, length us, event | category | flops | bytes accessed | tf_op | source)
XLA Modules:
  0.0 154.0 jit_solution(11493722510023593171)
XLA Ops:
  0.1 0.1 fusion.4
  0.2 0.7 and_select_fusion
  0.9 2.0 %sort.34 = (s32[64]{0:T(128)}, s32[64]{0:T(128)S(1)}) sort(s32[64]{0:T(128)S(1)} %get-tuple-element.21, s32[64]{0:T(128)S(1)} %iota.34), dimensions={0}, to_apply=%region_0.1 | sort | flops 384 | bytes 1024 | tf_op jit(solution)/shard_map/jit(argsort)/sort | solution.py:422
  3.0 0.8 gather_fusion.1
  3.7 0.1 reshape.110
  3.8 0.1 broadcast_in_dim.9.cosines
  3.9 0.7 broadcast_multiply_fusion.1
  4.7 0.8 copy.11
  5.4 0.1 reshape.111.child
  5.5 0.3 fusion
  6.0 0.0 copy-start.4
  6.0 0.0 copy-start.5
  6.0 0.0 copy-start.6
  6.0 5.0 %gather_fusion = f32[64,128,128]{2,1,0:T(8,128)} fusion(f32[64,128,128]{2,1,0:T(8,128)} %bitcast.14, s32[1024]{0:T(1024)S(1)} %pad_clamp_fusion), kind=kCustom, calls=%fused_computation | custom fusion | bytes 8388864 | tf_op jit(solution)/shard_map/gather | solution.py:424
  11.0 0.0 copy-done.4
  11.0 0.0 copy-done.5
  11.0 0.0 copy-done.6
  11.1 0.0 copy-start.2
  11.1 2.2 %copy-done.2 = f32[64,128,128]{2,1,0:T(8,128)S(1)} copy-done((f32[64,128,128]{2,1,0:T(8,128)S(1)}, f32[64,128,128]{2,1,0:T(8,128)}, u32[]{:S(2)}) %copy-start.2) | copy-done | bytes 4194328
  13.2 0.0 copy-start.3
  13.2 115.7 %exchange.1 = (f32[8,8,8,16,128]{4,3,2,1,0:T(8,128)S(1)}, s32[8,1,128]{2,1,0:T(1,128)S(1)}) custom-call(f32[8,8,128,128]{3,2,1,0:T(8,128)S(1)} %bitcast.11, s32[8,1,128]{2,1,0:T(1,128)S(1)} %pad.4.slots, f32[16,128]{1,0:T(8,128)S(1)} %get-tuple-element.22.diag, f32[16,128]{1,0:T(8,128)S(1)} %broadcast_in_dim.9.cosines, f32[1,128]{1,0:T(1,128)S(1)} %copy-done.6, ...), custom_call_target="tpu_custom_call" | custom-call | tf_op jit(solution)/shard_map/exchange/pallas_call | solution.py:379
  128.9 0.0 copy-start
  128.9 2.0 %copy-done = f32[8,8,8,16,128]{4,3,2,1,0:T(8,128)} copy-done((f32[8,8,8,16,128]{4,3,2,1,0:T(8,128)}, f32[8,8,8,16,128]{4,3,2,1,0:T(8,128)S(1)}, u32[]{:S(2)}) %copy-start) | copy-done | bytes 4194328
  131.0 0.1 reshape_squeeze.3
  131.0 2.1 %sort.35 = (s32[64]{0:T(128)}, s32[64]{0:T(128)S(1)}) sort(s32[64]{0:T(128)S(1)} %reshape_squeeze.3, s32[64]{0:T(128)S(1)} %iota.36), dimensions={0}, to_apply=%region_1.2 | sort | flops 384 | bytes 1024 | tf_op jit(solution)/shard_map/jit(argsort)/sort | solution.py:429
  133.2 0.0 copy-done.3
  133.2 0.0 copy-start.1
  133.2 2.2 %copy-done.1 = f32[8,8,8,16,128]{4,3,2,1,0:T(8,128)S(1)} copy-done((f32[8,8,8,16,128]{4,3,2,1,0:T(8,128)S(1)}, f32[8,8,8,16,128]{4,3,2,1,0:T(8,128)}, u32[]{:S(2)}) %copy-start.1) | copy-done | bytes 4194328
  135.4 18.6 %transform.1 = f32[64,4,8,32,128]{4,3,2,1,0:T(8,128)} custom-call(s32[64]{0:T(128)S(1)} %get-tuple-element.11.source, s32[512]{0:T(512)S(1)} %reshape.111.child, f32[64,8,16,128]{3,2,1,0:T(8,128)S(1)} %bitcast.7, f32[64,8,16,128]{3,2,1,0:T(8,128)S(1)} %bitcast.8, f32[64,8,16,128]{3,2,1,0:T(8,128)S(1)} %bitcast.9, f32[64,8,16,128]{3,2,1,0:T(8,128)S(1)} %bitcast.10, ...), custom_call_target="tpu_custom_call" | custom-call | tf_op jit(solution)/shard_map/transform/pallas_call | solution.py:137
  (13 shorter events, 0.2 us)
Async XLA Ops:
  6.0 5.1 %copy-start.4 = (f32[64,1,128]{2,1,0:T(1,128)S(1)}, f32[64,1,128]{2,1,0:T(1,128)}, u32[]{:S(2)}) copy-start(f32[64,1,128]{2,1,0:T(1,128)} %constant.69.clone.before) | copy-start | bytes 98308
  6.0 5.1 %copy-start.5 = (f32[64,1,128]{2,1,0:T(1,128)S(1)}, f32[64,1,128]{2,1,0:T(1,128)}, u32[]{:S(2)}) copy-start(f32[64,1,128]{2,1,0:T(1,128)} %constant.68.clone.factor) | copy-start | bytes 98308
  6.0 5.0 %copy-start.6 = (f32[1,128]{1,0:T(1,128)S(1)}, f32[1,128]{1,0:T(1,128)}, u32[]{:S(2)}) copy-start(f32[1,128]{1,0:T(1,128)} %constant.66.clone.orders) | copy-start | bytes 1540
  11.1 2.2 %copy-start.2 = (f32[64,128,128]{2,1,0:T(8,128)S(1)}, f32[64,128,128]{2,1,0:T(8,128)}, u32[]{:S(2)}) copy-start(f32[64,128,128]{2,1,0:T(8,128)} %gather_fusion) | copy-start | bytes 12582916
  13.2 119.9 %copy-start.3 = (f32[256,256]{1,0:T(8,128)S(1)}, f32[256,256]{1,0:T(8,128)}, u32[]{:S(2)}) copy-start(f32[256,256]{1,0:T(8,128)} %constant.70.clone.refs_4_) | copy-start | bytes 786436
  128.9 2.0 %copy-start = (f32[8,8,8,16,128]{4,3,2,1,0:T(8,128)}, f32[8,8,8,16,128]{4,3,2,1,0:T(8,128)S(1)}, u32[]{:S(2)}) copy-start(f32[8,8,8,16,128]{4,3,2,1,0:T(8,128)S(1)} %get-tuple-element.12) | copy-start | bytes 12582916
  133.2 2.2 %copy-start.1 = (f32[8,8,8,16,128]{4,3,2,1,0:T(8,128)S(1)}, f32[8,8,8,16,128]{4,3,2,1,0:T(8,128)}, u32[]{:S(2)}) copy-start(f32[8,8,8,16,128]{4,3,2,1,0:T(8,128)} %copy-done) | copy-start | bytes 12582916
